TPU v7x, 512 devices: a whole 4x8x8 slice. The times are simulated.
512 devices in a mesh: lrow: 8 (over z), rcol: 16 (over x, y_lo, core), term: 4 (over y_hi).
Axes of the slice: x: 4, y: 8 (y_hi: 4, y_lo: 2; y = y_hi * 2 + y_lo), z: 8, core: 2. Of those that a mesh axis runs over, the one named last changes fastest.
Arguments:
- core_left: bfloat16 [256, 256, 128], P(None, 'rcol'), may hold values from -6 to 6
- core_right: bfloat16 [256, 256, 128], P('rcol', 'lrow'), may hold values from -0.03125 to 0.03125
- env_left: bfloat16 [20, 32, 256], P('term', 'lrow'), may hold values from -0.375 to 0.375
- env_right: bfloat16 [20, 256, 256], P('term'), may hold values from -0.375 to 0.375
- coef_left: float32 [20, 3, 128], P('term'), may hold values from -1.5 to 1.5
- coef_right: float32 [20, 3, 128], P('term'), may hold values from -1.5 to 1.5
- projected: bfloat16 [128, 32, 256, 128], P('term', 'lrow', 'rcol'), may hold values from -6 to 6
Outputs:
- residual: bfloat16 [128, 32, 256, 128], P('term', 'lrow', 'rcol')
All inputs are finite; a program needn't handle non-finite values.
Results may differ from a plain program's by a relative error of at most 0.012.
Values may be sent and summed in bfloat16 or wider, within the bound.
No kernel may reach another device: no remote copies, remote signals or barrier semaphores. Data moves between devices by JAX's collectives and lax.ppermute only.
A program may use at most 64 MiB of HBM per device.

v0:
```python
import jax
import jax.numpy as jnp
from jax import lax
from jax.sharding import PartitionSpec as P


def stencil_terms(field, coef):
    wide = field.astype(jnp.float32)
    zero = jnp.zeros_like(wide[..., :1])
    before = jnp.concatenate([zero, wide[..., :-1]], axis=-1)
    after = jnp.concatenate([wide[..., 1:], zero], axis=-1)
    scaled = coef[:, :, None, None, :]
    return scaled[:, 0] * wide[None] + scaled[:, 1] * before[None] + scaled[:, 2] * after[None]


def on_device(core_left, core_right, env_left, env_right, coef_left, coef_right, projected):
    left_field = stencil_terms(core_left, coef_left).astype(jnp.bfloat16)
    left_frame = jnp.einsum(
        "tpq,tqrs->trps", env_left, left_field, preferred_element_type=jnp.float32
    ).astype(jnp.bfloat16)
    left_frame = lax.all_gather(left_frame, "rcol", axis=1, tiled=True)
    right_block = lax.all_gather(core_right, "lrow", axis=1, tiled=True)
    right_field = stencil_terms(right_block, coef_right).astype(jnp.bfloat16)
    right_frame = jnp.einsum(
        "tbq,trqj->trbj", env_right, right_field, preferred_element_type=jnp.float32
    ).astype(jnp.bfloat16)
    partial_sum = jnp.einsum(
        "trai,trbj->jabi",
        left_frame,
        lax.all_to_all(right_frame, "rcol", split_axis=2, concat_axis=1, tiled=True),
        preferred_element_type=jnp.float32,
    )
    summed = lax.psum_scatter(
        partial_sum.astype(jnp.bfloat16), "term", scatter_dimension=0, tiled=True
    ).astype(jnp.float32)
    return (projected.astype(jnp.float32) - summed).astype(jnp.bfloat16)


def solution(mesh):
    return jax.shard_map(
        on_device,
        mesh=mesh,
        in_specs=(
            P(None, "rcol", None),
            P("rcol", "lrow", None),
            P("term", "lrow", None),
            P("term", None, None),
            P("term", None, None),
            P("term", None, None),
            P("term", "lrow", "rcol", None),
        ),
        out_specs=P("term", "lrow", "rcol", None),
        check_vma=False,
    )
```

profile of v0, /device:TPU:20, one launch (start us, length us, event | category | flops | bytes accessed | tf_op | source)
XLA Modules:
  0.0 234.9 jit_solution(17720216909429817425)
XLA Ops:
  7.4 0.0 copy-start
  7.4 0.0 all-gather.3.cloned.1.call-start
  7.4 0.7 all-gather.3.cloned.1.call-update
  8.1 0.8 fusion.24
  8.9 48.0 %all-gather.3.cloned.1.call-done = bf16[16,256,128]{2,1,0:T(8,128)(2,1)} async-done(((bf16[16,32,128]{2,1,0:T(8,128)(2,1)}), bf16[16,256,128]{2,1,0:T(8,128)(2,1)}) %all-gather.3.cloned.1.call-update) | async-done | bytes 1048592 | tf_op jit(solution)/shard_map/all_gather | solution.py:22
  56.9 3.4 %fusion.22 = (f32[16,256,127]{2,1,0:T(8,128)}, f32[16,256,127]{2,1,0:T(8,128)S(1)}) fusion(bf16[16,256,128]{2,1,0:T(8,128)(2,1)} %all-gather.3.cloned.1.call-done), kind=kLoop, calls=%fused_computation.29 | loop fusion | bytes 8323072 | tf_op jit(solution)/shard_map/slice | solution.py:10
  60.3 2.9 %copy.48 = f32[16,256,127]{1,2,0:T(8,128)} copy(f32[16,256,127]{2,1,0:T(8,128)} %get-tuple-element.7) | data formatting | bytes 4161536
  63.3 1.9 copy.49
  65.2 0.0 copy-start.2
  65.2 2.0 concatenate.12.clone
  67.1 0.3 copy-done.2
  67.4 1.5 concatenate.13.clone
  68.9 2.7 %copy.23 = f32[16,256,128]{1,2,0:T(8,128)} copy(bf16[16,256,128]{2,1,0:T(8,128)(2,1)} %all-gather.3.cloned.1.call-done) | data formatting | bytes 3145728 | tf_op jit(solution)/shard_map/convert_element_type | solution.py:8
  71.5 0.0 copy-done
  71.5 5.8 %convert_bitcast_fusion = bf16[5,16,256,128]{2,3,1,0:T(8,128)(2,1)} fusion(f32[16,256,128]{1,2,0:T(8,128)} %concatenate.13.clone, f32[5,128]{1,0:T(8,128)S(1)} %get-tuple-element.15, f32[16,256,128]{1,2,0:T(8,128)S(1)} %concatenate.12.clone, f32[5,128]{1,0:T(8,128)S(1)} %get-tuple-element.16, f32[16,256,128]{1,2,0:T(8,128)} %copy.23, ...), kind=kOutput, calls=%fused_computation.5 | convolution fusion | flops 1360527360 | bytes 12197376 | tf_op jit(solution)/shard_map/tbq,trqj->trbj/dot_general | solution.py:24
  77.3 8.3 %copy.26 = bf16[5,16,256,128]{3,1,0,2:T(8,128)(2,1)} copy(bf16[5,16,256,128]{2,3,1,0:T(8,128)(2,1)} %convert_bitcast_fusion) | data formatting | bytes 10485760 | tf_op jit(solution)/shard_map/convert_element_type | solution.py:26
  85.6 0.0 copy-start.4
  85.6 0.0 copy-start.1
  85.6 5.9 %all-to-all-start = ((bf16[5,16,256,128]{3,1,0,2:T(8,128)(2,1)}), bf16[5,16,256,128]{3,1,0,2:T(8,128)(2,1)}, u32[]{:S(2)}, u32[]{:S(2)}) async-start(bf16[5,16,256,128]{3,1,0,2:T(8,128)(2,1)} %copy.26), calls=%async_computation | async-start | bytes 10485760 | tf_op jit(solution)/shard_map/all_to_all | solution.py:30
  91.5 0.0 all-gather.5.cloned.1.call-start
  91.5 0.0 copy-done.4
  91.6 0.0 copy-done.1
  91.6 0.2 copy.29
  91.8 0.4 fusion.21
  92.3 0.7 copy.50
  92.9 0.6 concatenate.14.clone
  93.6 0.0 copy-start.5
  93.6 0.7 copy.51
  94.2 0.2 concatenate.15.clone
  94.4 0.0 copy-done.5
  94.5 2.8 %fusion.18 = bf16[5,16,4,128]{3,2,1,0:T(4,128)(2,1)} fusion(f32[256,16,128]{2,0,1:T(8,128)S(1)} %concatenate.15.clone, f32[5,128]{1,0:T(8,128)S(1)} %get-tuple-element.17, f32[256,16,128]{2,0,1:T(8,128)S(1)} %concatenate.14.clone, f32[5,128]{1,0:T(8,128)S(1)} %get-tuple-element.18, f32[256,16,128]{2,0,1:T(8,128)S(1)} %copy.29, f32[5,128]{1,0:T(8,128)S(1)} %bitcast.50, ...), kind=kOutput, calls=%fused_computation.18 | convolution fusion | flops 36741120 | bytes 6391296 | tf_op jit(solution)/shard_map/tpq,tqrs->trps/dot_general | solution.py:18
  97.2 0.0 all-gather.5.cloned.1.call-update
  97.3 0.2 reduce-scatter.2.cloned.1.call-start
  97.5 56.7 %all-to-all-done = bf16[5,16,256,128]{3,1,0,2:T(8,128)(2,1)} async-done(((bf16[5,16,256,128]{3,1,0,2:T(8,128)(2,1)}), bf16[5,16,256,128]{3,1,0,2:T(8,128)(2,1)}, u32[]{:S(2)}, u32[]{:S(2)}) %all-to-all-start) | async-done | bytes 5242912 | tf_op jit(solution)/shard_map/all_to_all | solution.py:30
  154.2 6.2 %copy.28 = bf16[5,16,16,16,128]{4,3,2,1,0:T(8,128)(2,1)} copy(bf16[5,16,16,16,128]{4,2,0,3,1:T(8,128)(2,1)} %bitcast.6) | data formatting | bytes 10485760 | tf_op jit(solution)/shard_map/all_to_all | solution.py:30
  160.4 5.9 %all-gather.5.cloned.1.call-done = bf16[5,256,4,128]{3,2,1,0:T(4,128)(2,1)} async-done(((bf16[5,16,4,128]{3,2,1,0:T(4,128)(2,1)}), bf16[5,256,4,128]{3,2,1,0:T(4,128)(2,1)}) %all-gather.5.cloned.1.call-update) | async-done | bytes 1310736 | tf_op jit(solution)/shard_map/all_gather | solution.py:21
  166.3 0.0 copy-start.3
  166.3 7.7 %fusion.12 = bf16[128,4,16,128]{3,0,1,2:T(8,128)(2,1)} fusion(bf16[5,256,16,128,1]{3,2,1,0,4:T(8,128)(2,1)} %bitcast.46, bf16[5,256,4,128]{3,2,1,0:T(4,128)(2,1)} %all-gather.5.cloned.1.call-done), kind=kOutput, calls=%fused_computation.14 | convolution fusion | flops 2685403136 | bytes 8650752 | tf_op jit(solution)/shard_map/trai,trbj->jabi/dot_general | solution.py:27
  174.0 0.0 reduce-scatter.2.cloned.1.call-update
  174.0 50.9 %reduce-scatter.2.cloned.1.call-done = bf16[32,4,16,128]{3,0,1,2:T(8,128)(2,1)} async-done(((bf16[128,4,16,128]{3,0,1,2:T(8,128)(2,1)}), bf16[32,4,16,128]{3,0,1,2:T(8,128)(2,1)}) %reduce-scatter.2.cloned.1.call-update) | async-done | bytes 524304 | tf_op jit(solution)/shard_map/reduce_scatter | solution.py:33
  225.0 0.0 copy-done.3
  225.0 1.4 subtract_convert_fusion
  226.4 1.1 copy.34
  (5 shorter events, 0.0 us)
Async XLA Ops:
  7.4 64.2 %copy-start = (bf16[5,256,256]{2,1,0:T(8,128)(2,1)S(1)}, bf16[5,256,256]{2,1,0:T(8,128)(2,1)}, u32[]{:S(2)}) copy-start(bf16[5,256,256]{2,1,0:T(8,128)(2,1)} %param.10) | copy-start | bytes 1966084
  7.4 49.6 %all-gather.3.cloned.1.call-start = ((), (), s32[]{:S(2)}) async-start(), calls=%async_computation.2 | async-start | bytes 1179648 | tf_op jit(solution)/shard_map/all_gather | solution.py:22
  65.2 2.2 copy-start.2
  85.6 5.9 %copy-start.4 = (f32[5,3,128]{2,1,0:T(4,128)S(1)}, f32[5,3,128]{2,1,0:T(4,128)}, u32[]{:S(2)}) copy-start(f32[5,3,128]{2,1,0:T(4,128)} %param.11) | copy-start | bytes 23044
  85.6 6.0 %copy-start.1 = (bf16[256,16,128]{2,1,0:T(8,128)(2,1)S(1)}, bf16[256,16,128]{2,1,0:T(8,128)(2,1)}, u32[]{:S(2)}) copy-start(bf16[256,16,128]{2,1,0:T(8,128)(2,1)} %param.7) | copy-start | bytes 3145732
  85.6 68.6 %all-to-all-start = ((bf16[5,16,256,128]{3,1,0,2:T(8,128)(2,1)}), bf16[5,16,256,128]{3,1,0,2:T(8,128)(2,1)}, u32[]{:S(2)}, u32[]{:S(2)}) async-start(bf16[5,16,256,128]{3,1,0,2:T(8,128)(2,1)} %copy.26), calls=%async_computation | async-start | bytes 10485760 | tf_op jit(solution)/shard_map/all_to_all | solution.py:30
  91.5 74.9 %all-gather.5.cloned.1.call-start = ((), (), s32[]{:S(2)}) async-start(), calls=%async_computation.3 | async-start | bytes 1392640 | tf_op jit(solution)/shard_map/all_gather | solution.py:21
  93.6 0.9 copy-start.5
  97.3 127.7 %reduce-scatter.2.cloned.1.call-start = ((), (), s32[]{:S(2)}) async-start(), calls=%async_computation.4 | async-start | bytes 2621440 | tf_op jit(solution)/shard_map/reduce_scatter | solution.py:33
  166.3 58.6 %copy-start.3 = (bf16[32,4,16,128]{3,2,1,0:T(8,128)(2,1)S(1)}, bf16[32,4,16,128]{3,2,1,0:T(8,128)(2,1)}, u32[]{:S(2)}) copy-start(bf16[32,4,16,128]{3,2,1,0:T(8,128)(2,1)} %param.13) | copy-start | bytes 1572868
Sparse Core Ops, SparseCore 0:
  10.3 46.6 all-gather.2
  174.2 50.7 reduce-scatter.1
Sparse Core Ops, SparseCore 1:
  97.3 68.9 all-gather.4
where the time goes:
time: 235 us
  waiting for transfers between devices  162 us (69%)
  local copies, waits for them, and re-layouts  33.9 us (14%)
  matrix products  16.2 us (7%)
  between operations  15 us (6%)
  starting transfers between devices  6.14 us (3%)
    all_to_all x1, waiting for transfers between devices, on_device(): lax.all_to_all(right_frame, 'rcol', split_axis=2, concat_axis=1, tiled=True)  56.7 us
    reduce_scatter x1, waiting for transfers between devices, on_device(): lax.psum_scatter(partial_sum.astype(jnp.bfloat16), 'term', scatter_dimens...  50.9 us
    all_gather x1, waiting for transfers between devices, on_device(): right_block = lax.all_gather(core_right, 'lrow', axis=1, tiled=True)  48 us
    convert_element_type x1, local copies, waits for them, and re-layouts, on_device(): right_frame = jnp.einsum('tbq,trqj->trbj', env_right, right_field, prefer...  8.27 us
    dot_general x1, matrix products, on_device(): jnp.einsum('trai,trbj->jabi', left_frame, lax.all_to_all(right_frame, 'rc...  7.67 us
    unnamed x20, local copies, waits for them, and re-layouts  6.47 us
    all_to_all x1, local copies, waits for them, and re-layouts, on_device(): lax.all_to_all(right_frame, 'rcol', split_axis=2, concat_axis=1, tiled=True)  6.24 us
    all_gather x1, waiting for transfers between devices, on_device(): left_frame = lax.all_gather(left_frame, 'rcol', axis=1, tiled=True)  5.91 us
  transfers between devices with their start and end apart: 4, of which 4 were waited for; matrix products, arithmetic and copies ran while one was open for 5% of the time, Pallas kernels for 0%

commit v1 on v0

--- a/solution.py
+++ b/solution.py
@@ -2,6 +2,7 @@
 import jax.numpy as jnp
 from jax import lax
 from jax.sharding import PartitionSpec as P
+from jax.lax import all_to_all, axis_size
 
 
 def stencil_terms(field, coef):
@@ -19,7 +20,14 @@
         "tpq,tqrs->trps", env_left, left_field, preferred_element_type=jnp.float32
     ).astype(jnp.bfloat16)
     left_frame = lax.all_gather(left_frame, "rcol", axis=1, tiled=True)
-    right_block = lax.all_gather(core_right, "lrow", axis=1, tiled=True)
+    wide_n = axis_size("lrow")
+    right_block = all_to_all(
+        jnp.tile(core_right, [wide_n if k0 == 1 else 1 for k0 in range(core_right.ndim)]),
+        axis_name="lrow",
+        split_axis=1,
+        concat_axis=1,
+        tiled=True,
+    )
     right_field = stencil_terms(right_block, coef_right).astype(jnp.bfloat16)
     right_frame = jnp.einsum(
         "tbq,trqj->trbj", env_right, right_field, preferred_element_type=jnp.float32

time: 235 us -> 225 us (0.957)
  the two profiles are of different devices: /device:TPU:20 before, /device:TPU:22 now
where the time goes in v1:
time: 225 us
  waiting for transfers between devices  140 us (62%)
  local copies, waits for them, and re-layouts  36.4 us (16%)
  starting transfers between devices  16.5 us (7%)
  matrix products  16.5 us (7%)
  between operations  13.6 us (6%)
    all_to_all x1, waiting for transfers between devices, on_device(): lax.all_to_all(right_frame, 'rcol', split_axis=2, concat_axis=1, tiled=True)  57.2 us
    reduce_scatter x1, waiting for transfers between devices, on_device(): lax.psum_scatter(partial_sum.astype(jnp.bfloat16), 'term', scatter_dimens...  51 us
    all_to_all x1, waiting for transfers between devices, on_device(): all_to_all(jnp.tile(core_right, [wide_n if k0 == 1 else 1 for k0 in range...  28.7 us
    all_to_all x1, starting transfers between devices, on_device(): all_to_all(jnp.tile(core_right, [wide_n if k0 == 1 else 1 for k0 in range...  10.3 us
    convert_element_type x1, local copies, waits for them, and re-layouts, on_device(): right_frame = jnp.einsum('tbq,trqj->trbj', env_right, right_field, prefer...  8.27 us
    dot_general x1, matrix products, on_device(): jnp.einsum('trai,trbj->jabi', left_frame, lax.all_to_all(right_frame, 'rc...  7.68 us
    unnamed x22, local copies, waits for them, and re-layouts  7.38 us
    all_to_all x1, local copies, waits for them, and re-layouts, on_device(): lax.all_to_all(right_frame, 'rcol', split_axis=2, concat_axis=1, tiled=True)  6.2 us
  transfers between devices with their start and end apart: 4, of which 4 were waited for; matrix products, arithmetic and copies ran while one was open for 5% of the time, Pallas kernels for 0%

profile of v1, /device:TPU:22, one launch (start us, length us, event | category | flops | bytes accessed | tf_op | source)
XLA Modules:
  0.0 224.5 jit_solution(13350860599251104618)
XLA Ops:
  6.5 0.0 copy-start
  6.5 0.0 copy-start.4
  6.5 1.1 tile.4
  7.7 1.7 copy.21
  9.4 10.3 %all-to-all-start = ((bf16[16,256,128]{2,0,1:T(8,128)(2,1)}), bf16[16,256,128]{2,0,1:T(8,128)(2,1)S(1)}, u32[]{:S(2)}, u32[]{:S(2)}) async-start(bf16[16,256,128]{2,0,1:T(8,128)(2,1)} %copy.21), calls=%async_computation | async-start | bytes 2097152 | tf_op jit(solution)/shard_map/all_to_all | solution.py:24
  19.7 0.0 copy-done.4
  19.7 28.7 %all-to-all-done = bf16[16,256,128]{2,0,1:T(8,128)(2,1)S(1)} async-done(((bf16[16,256,128]{2,0,1:T(8,128)(2,1)}), bf16[16,256,128]{2,0,1:T(8,128)(2,1)S(1)}, u32[]{:S(2)}, u32[]{:S(2)}) %all-to-all-start) | async-done | bytes 1048608 | tf_op jit(solution)/shard_map/all_to_all | solution.py:24
  48.4 2.5 %fusion.22 = (f32[16,256,127]{2,0,1:T(8,128)}, f32[16,256,127]{2,0,1:T(8,128)}) fusion(bf16[16,256,128]{2,0,1:T(8,128)(2,1)S(1)} %all-to-all-done), kind=kLoop, calls=%fused_computation.29 | loop fusion | bytes 8323072 | tf_op jit(solution)/shard_map/slice | solution.py:11
  50.9 2.9 %copy.47 = f32[16,256,127]{1,2,0:T(8,128)} copy(f32[16,256,127]{2,0,1:T(8,128)} %get-tuple-element.7) | data formatting | bytes 4161536
  53.8 3.0 %copy.48 = f32[16,256,127]{1,2,0:T(8,128)} copy(f32[16,256,127]{2,0,1:T(8,128)} %get-tuple-element.8) | data formatting | bytes 4161536
  56.9 0.0 copy-start.2
  56.9 3.3 %concatenate.12.clone = f32[16,256,128]{1,2,0:T(8,128)} pad(f32[16,256,127]{1,2,0:T(8,128)} %copy.47, f32[]{:T(128)} %constant.1.clone.1), padding=0_0x0_0x1_0 | pad | bytes 4177924 | tf_op jit(solution)/shard_map/concatenate | solution.py:11
  60.2 0.0 copy-done.2
  60.2 1.6 concatenate.13.clone
  61.7 1.8 copy.22
  63.5 0.0 copy-done
  63.5 6.1 %convert_bitcast_fusion = bf16[5,16,256,128]{2,3,1,0:T(8,128)(2,1)} fusion(f32[16,256,128]{1,2,0:T(8,128)} %concatenate.13.clone, f32[5,128]{1,0:T(8,128)S(1)} %get-tuple-element.15, f32[16,256,128]{1,2,0:T(8,128)} %concatenate.12.clone, f32[5,128]{1,0:T(8,128)S(1)} %get-tuple-element.16, f32[16,256,128]{1,2,0:T(8,128)} %copy.22, f32[5,128]{1,0:T(8,128)S(1)} %bitcast.49, ...), kind=kOutput, calls=%fused_computation.5 | convolution fusion | flops 1360527360 | bytes 12197376 | tf_op jit(solution)/shard_map/tbq,trqj->trbj/dot_general | solution.py:32
  69.6 8.3 %copy.25 = bf16[5,16,256,128]{3,1,0,2:T(8,128)(2,1)} copy(bf16[5,16,256,128]{2,3,1,0:T(8,128)(2,1)} %convert_bitcast_fusion) | data formatting | bytes 10485760 | tf_op jit(solution)/shard_map/convert_element_type | solution.py:34
  77.9 0.0 copy-start.5
  77.9 0.0 copy-start.1
  77.9 5.9 %all-to-all-start.1 = ((bf16[5,16,256,128]{3,1,0,2:T(8,128)(2,1)}), bf16[5,16,256,128]{3,1,0,2:T(8,128)(2,1)}, u32[]{:S(2)}, u32[]{:S(2)}) async-start(bf16[5,16,256,128]{3,1,0,2:T(8,128)(2,1)} %copy.25), calls=%async_computation.1 | async-start | bytes 10485760 | tf_op jit(solution)/shard_map/all_to_all | solution.py:38
  83.8 0.0 all-gather.2.cloned.1.call-start
  83.9 0.0 copy-done.5
  83.9 0.0 copy-done.1
  83.9 0.2 copy.28
  84.2 0.4 fusion.21
  84.6 0.7 copy.49
  85.3 0.6 concatenate.14.clone
  85.9 0.0 copy-start.6
  85.9 0.7 copy.50
  86.6 0.2 concatenate.15.clone
  86.8 0.0 copy-done.6
  86.8 2.8 %fusion.18 = bf16[5,16,4,128]{3,2,1,0:T(4,128)(2,1)} fusion(f32[256,16,128]{2,0,1:T(8,128)S(1)} %concatenate.15.clone, f32[5,128]{1,0:T(8,128)S(1)} %get-tuple-element.17, f32[256,16,128]{2,0,1:T(8,128)S(1)} %concatenate.14.clone, f32[5,128]{1,0:T(8,128)S(1)} %get-tuple-element.18, f32[256,16,128]{2,0,1:T(8,128)S(1)} %copy.28, f32[5,128]{1,0:T(8,128)S(1)} %bitcast.52, ...), kind=kOutput, calls=%fused_computation.18 | convolution fusion | flops 36741120 | bytes 6391296 | tf_op jit(solution)/shard_map/tpq,tqrs->trps/dot_general | solution.py:19
  89.6 0.0 all-gather.2.cloned.1.call-update
  89.6 0.2 reduce-scatter.2.cloned.1.call-start
  89.9 57.2 %all-to-all-done.1 = bf16[5,16,256,128]{3,1,0,2:T(8,128)(2,1)} async-done(((bf16[5,16,256,128]{3,1,0,2:T(8,128)(2,1)}), bf16[5,16,256,128]{3,1,0,2:T(8,128)(2,1)}, u32[]{:S(2)}, u32[]{:S(2)}) %all-to-all-start.1) | async-done | bytes 5242912 | tf_op jit(solution)/shard_map/all_to_all | solution.py:38
  147.0 6.2 %copy.27 = bf16[5,16,16,16,128]{4,3,2,1,0:T(8,128)(2,1)} copy(bf16[5,16,16,16,128]{4,2,0,3,1:T(8,128)(2,1)} %bitcast.7) | data formatting | bytes 10485760 | tf_op jit(solution)/shard_map/all_to_all | solution.py:38
  153.2 3.2 %all-gather.2.cloned.1.call-done = bf16[5,256,4,128]{3,2,1,0:T(4,128)(2,1)} async-done(((bf16[5,16,4,128]{3,2,1,0:T(4,128)(2,1)}), bf16[5,256,4,128]{3,2,1,0:T(4,128)(2,1)}) %all-gather.2.cloned.1.call-update) | async-done | bytes 1310736 | tf_op jit(solution)/shard_map/all_gather | solution.py:22
  156.4 0.0 copy-start.3
  156.4 7.7 %fusion.12 = bf16[128,4,16,128]{3,0,1,2:T(8,128)(2,1)} fusion(bf16[5,256,16,128,1]{3,2,1,0,4:T(8,128)(2,1)} %bitcast.47, bf16[5,256,4,128]{3,2,1,0:T(4,128)(2,1)} %all-gather.2.cloned.1.call-done), kind=kOutput, calls=%fused_computation.14 | convolution fusion | flops 2685403136 | bytes 8650752 | tf_op jit(solution)/shard_map/trai,trbj->jabi/dot_general | solution.py:35
  164.1 0.0 reduce-scatter.2.cloned.1.call-update
  164.1 51.0 %reduce-scatter.2.cloned.1.call-done = bf16[32,4,16,128]{3,0,1,2:T(8,128)(2,1)} async-done(((bf16[128,4,16,128]{3,0,1,2:T(8,128)(2,1)}), bf16[32,4,16,128]{3,0,1,2:T(8,128)(2,1)}) %reduce-scatter.2.cloned.1.call-update) | async-done | bytes 524304 | tf_op jit(solution)/shard_map/reduce_scatter | solution.py:41
  215.1 0.0 copy-done.3
  215.2 1.4 subtract_convert_fusion
  216.6 1.1 copy.33
  (6 shorter events, 0.0 us)
Async XLA Ops:
  6.5 57.0 %copy-start = (bf16[5,256,256]{2,1,0:T(8,128)(2,1)S(1)}, bf16[5,256,256]{2,1,0:T(8,128)(2,1)}, u32[]{:S(2)}) copy-start(bf16[5,256,256]{2,1,0:T(8,128)(2,1)} %param.10) | copy-start | bytes 1966084
  6.5 13.1 %copy-start.4 = (f32[5,3,128]{2,1,0:T(4,128)S(1)}, f32[5,3,128]{2,1,0:T(4,128)}, u32[]{:S(2)}) copy-start(f32[5,3,128]{2,1,0:T(4,128)} %param.12) | copy-start | bytes 23044
  9.4 39.0 %all-to-all-start = ((bf16[16,256,128]{2,0,1:T(8,128)(2,1)}), bf16[16,256,128]{2,0,1:T(8,128)(2,1)S(1)}, u32[]{:S(2)}, u32[]{:S(2)}) async-start(bf16[16,256,128]{2,0,1:T(8,128)(2,1)} %copy.21), calls=%async_computation | async-start | bytes 2097152 | tf_op jit(solution)/shard_map/all_to_all | solution.py:24
  56.9 3.3 %copy-start.2 = (f32[16,256,127]{1,2,0:T(8,128)S(1)}, f32[16,256,127]{1,2,0:T(8,128)}, u32[]{:S(2)}) copy-start(f32[16,256,127]{1,2,0:T(8,128)} %copy.48) | copy-start | bytes 6242308
  77.9 6.0 %copy-start.5 = (f32[5,3,128]{2,1,0:T(4,128)S(1)}, f32[5,3,128]{2,1,0:T(4,128)}, u32[]{:S(2)}) copy-start(f32[5,3,128]{2,1,0:T(4,128)} %param.11) | copy-start | bytes 23044
  77.9 6.0 %copy-start.1 = (bf16[256,16,128]{2,1,0:T(8,128)(2,1)S(1)}, bf16[256,16,128]{2,1,0:T(8,128)(2,1)}, u32[]{:S(2)}) copy-start(bf16[256,16,128]{2,1,0:T(8,128)(2,1)} %param.7) | copy-start | bytes 3145732
  77.9 69.1 %all-to-all-start.1 = ((bf16[5,16,256,128]{3,1,0,2:T(8,128)(2,1)}), bf16[5,16,256,128]{3,1,0,2:T(8,128)(2,1)}, u32[]{:S(2)}, u32[]{:S(2)}) async-start(bf16[5,16,256,128]{3,1,0,2:T(8,128)(2,1)} %copy.25), calls=%async_computation.1 | async-start | bytes 10485760 | tf_op jit(solution)/shard_map/all_to_all | solution.py:38
  83.8 72.6 %all-gather.2.cloned.1.call-start = ((), (), s32[]{:S(2)}) async-start(), calls=%async_computation.3 | async-start | bytes 1392640 | tf_op jit(solution)/shard_map/all_gather | solution.py:22
  85.9 0.9 copy-start.6
  89.6 125.5 %reduce-scatter.2.cloned.1.call-start = ((), (), s32[]{:S(2)}) async-start(), calls=%async_computation.4 | async-start | bytes 2621440 | tf_op jit(solution)/shard_map/reduce_scatter | solution.py:41
  156.4 58.7 %copy-start.3 = (bf16[32,4,16,128]{3,2,1,0:T(8,128)(2,1)S(1)}, bf16[32,4,16,128]{3,2,1,0:T(8,128)(2,1)}, u32[]{:S(2)}) copy-start(bf16[32,4,16,128]{3,2,1,0:T(8,128)(2,1)} %param.13) | copy-start | bytes 1572868
Sparse Core Ops, SparseCore 0:
  89.7 66.6 all-gather.1
  164.2 50.8 reduce-scatter.1
